TPU v7x, 32 devices: a whole 2x2x4 slice. The times are simulated.
32 devices in a mesh: mom: 8 (over z, x), row: 2 (over core), col: 2 (over y).
Axes of the slice: x: 2, y: 2, z: 4, core: 2. Of those that a mesh axis runs over, the one named last changes fastest.
Arguments:
- left_part: bfloat16 [8, 1536, 1536], P('mom', 'row', 'col'), may hold values from -0.15625 to 0.15625
- vertex: bfloat16 [8, 1536, 1536], P('mom', 'row', 'col'), may hold values from -6 to 6
- bubble: float32 [8, 1536], P('mom'), may hold values from 0.25 to 2
- cross_map: int32 [1536, 8], P(('col', 'mom')), may hold values from 0 to 7, each once within a row
Outputs:
- crossed: bfloat16 [1536, 8, 1536], P(('col', 'mom'), None, 'row')
Inputs may be any that keep to these rules, and one draw needn't show every extreme that they name: Each row cross_map[b, :] is a permutation of the 8 transfer momenta.
All inputs are finite; a program needn't handle non-finite values.
Results may differ from a plain program's by a relative error of at most 0.0055.
Values may be sent and summed in bfloat16 or wider, within the bound.
No kernel may reach another device: no remote copies, remote signals or barrier semaphores. Data moves between devices by JAX's collectives and lax.ppermute only.
A program may use at most 64 MiB of HBM per device.

v0:
```python
import jax
import jax.numpy as jnp
from jax import lax
from jax.sharding import PartitionSpec as P


def on_device(left_part, vertex, bubble, cross_map):
    left_full = lax.all_gather(left_part, "col", axis=2, tiled=True)
    weighted = (left_full.astype(jnp.float32) * bubble[:, None, :]).astype(jnp.bfloat16)
    local_q = vertex.shape[0]
    col_count = vertex.shape[2]
    row_count = weighted.shape[1]
    momenta = lax.axis_size("mom")
    per_device = col_count // momenta
    sliced = weighted
    first_term = jnp.einsum(
        "qkb,qak->qba",
        lax.all_gather(vertex, "row", axis=1, tiled=True),
        sliced,
        preferred_element_type=jnp.float32,
    )
    first_round = first_term.astype(jnp.bfloat16)
    flipped = jnp.swapaxes(vertex, 1, 2).astype(jnp.float32)
    sliced = weighted
    second_term = jnp.einsum(
        "qbk,qak->qba",
        lax.all_gather(first_round, "row", axis=2, tiled=True),
        sliced,
        preferred_element_type=jnp.float32,
    )
    summed = (flipped + first_term + second_term).astype(jnp.bfloat16)
    summed = summed.reshape(local_q, momenta, per_device, row_count)
    received = lax.all_to_all(summed, "mom", split_axis=1, concat_axis=0, tiled=True)
    regrouped = received.reshape(-1, per_device, received.shape[-1])
    which = jnp.arange(per_device, dtype=jnp.int32)[:, None]
    return regrouped[cross_map, which]


def solution(mesh):
    in_specs = (
        P("mom", "row", "col"),
        P("mom", "row", "col"),
        P("mom", None),
        P(("col", "mom"), None),
    )
    out_specs = P(("col", "mom"), None, "row")
    return jax.shard_map(
        on_device, mesh=mesh, in_specs=in_specs, out_specs=out_specs, check_vma=False
    )
```

profile of v0, /device:TPU:0, one launch (start us, length us, event | category | flops | bytes accessed | tf_op | source)
XLA Modules:
  0.0 135.0 jit_solution(14771618672102993497)
XLA Ops:
  6.5 0.0 copy-start.1
  6.5 0.0 all-gather.5.cloned.1.call-start
  6.5 0.7 all-gather.5.cloned.1.call-update
  7.3 0.0 all-gather.7.cloned.1.call-start
  7.3 0.7 all-gather.7.cloned.1.call-update
  8.0 0.0 all-gather.9.cloned.1.call-start
  8.1 0.0 copy-done.1
  8.1 0.0 copy-start
  8.1 39.6 %all-gather.5.cloned.1.call-done = bf16[1,768,1536]{2,1,0:T(8,128)(2,1)} async-done(((bf16[1,768,768]{2,1,0:T(8,128)(2,1)}), bf16[1,768,1536]{2,1,0:T(8,128)(2,1)}) %all-gather.5.cloned.1.call-update) | async-done | bytes 2359312 | tf_op jit(solution)/shard_map/all_gather | solution.py:8
  47.7 12.5 %all-gather.7.cloned.1.call-done = bf16[1,1536,768]{2,1,0:T(8,128)(2,1)} async-done(((bf16[1,768,768]{2,1,0:T(8,128)(2,1)}), bf16[1,1536,768]{2,1,0:T(8,128)(2,1)}) %all-gather.7.cloned.1.call-update) | async-done | bytes 2359312 | tf_op jit(solution)/shard_map/all_gather | solution.py:18
  60.2 6.2 %bitcast_convert_fusion = (bf16[768,768]{1,0:T(8,128)(2,1)}, f32[768,768]{0,1:T(8,128)}) fusion(bf16[1,1536,768]{2,1,0:T(8,128)(2,1)} %all-gather.7.cloned.1.call-done, bf16[1,768,1536]{2,1,0:T(8,128)(2,1)} %all-gather.5.cloned.1.call-done, f32[1536]{0:T(1024)S(1)} %reduce), kind=kOutput, calls=%fused_computation.6 | convolution fusion | flops 1816068096 | bytes 8263680 | tf_op jit(solution)/shard_map/qkb,qak->qba/dot_general | solution.py:16
  66.4 0.0 all-gather.9.cloned.1.call-update
  66.5 0.0 copy-done
  66.5 0.6 copy.8
  67.1 11.6 %all-gather.9.cloned.1.call-done = bf16[768,1536]{1,0:T(8,128)(2,1)} async-done(((bf16[768,768]{1,0:T(8,128)(2,1)}), bf16[768,1536]{1,0:T(8,128)(2,1)}) %all-gather.9.cloned.1.call-update) | async-done | bytes 2359312 | tf_op jit(solution)/shard_map/all_gather | solution.py:27
  78.7 6.1 %fusion.2 = bf16[1,768,768]{2,1,0:T(8,128)(2,1)} fusion(f32[768,768]{0,1:T(8,128)} %get-tuple-element.6, bf16[1,768,768]{1,2,0:T(8,128)(2,1)S(1)} %copy.8, bf16[768,1536]{1,0:T(8,128)(2,1)} %all-gather.9.cloned.1.call-done, bf16[1,768,1536]{2,1,0:T(8,128)(2,1)} %all-gather.5.cloned.1.call-done, f32[1536]{0:T(1024)S(1)} %reduce), kind=kOutput, calls=%fused_computation.5 | convolution fusion | flops 1817837568 | bytes 9443328 | tf_op jit(solution)/shard_map/qbk,qak->qba/dot_general | solution.py:25
  84.9 0.0 copy-start.2
  84.9 5.9 %all-to-all-start = ((bf16[1,8,96,768]{3,2,0,1:T(8,128)(2,1)}), bf16[1,8,96,768]{3,2,0,1:T(8,128)(2,1)S(1)}, u32[]{:S(2)}, u32[]{:S(2)}) async-start(bf16[1,8,96,768]{3,2,0,1:T(8,128)(2,1)} %bitcast.7), calls=%async_computation | async-start | bytes 2359296 | tf_op jit(solution)/shard_map/all_to_all | solution.py:33
  90.8 0.0 copy-done.2
  90.8 0.1 copy.10
  90.9 0.1 reshape.33
  91.0 28.8 %all-to-all-done = bf16[1,8,96,768]{3,2,0,1:T(8,128)(2,1)S(1)} async-done(((bf16[1,8,96,768]{3,2,0,1:T(8,128)(2,1)}), bf16[1,8,96,768]{3,2,0,1:T(8,128)(2,1)S(1)}, u32[]{:S(2)}, u32[]{:S(2)}) %all-to-all-start) | async-done | bytes 1179680 | tf_op jit(solution)/shard_map/all_to_all | solution.py:33
  119.8 8.7 %gather_fusion = bf16[768,768]{1,0:T(8,128)(2,1)} fusion(bf16[8,96,768]{2,1,0:T(8,128)(2,1)S(1)} %bitcast.38, s32[768]{0:T(1024)S(1)} %reshape.33), kind=kCustom, calls=%fused_computation | custom fusion | bytes 2365440 | tf_op jit(solution)/shard_map/gather | solution.py:36
  (2 shorter events, 0.0 us)
Async XLA Ops:
  6.5 1.5 %copy-start.1 = (f32[1,1536]{1,0:T(1,128)S(1)}, f32[1,1536]{1,0:T(1,128)}, u32[]{:S(2)}) copy-start(f32[1,1536]{1,0:T(1,128)} %param.6) | copy-start | bytes 18436
  6.5 41.1 %all-gather.5.cloned.1.call-start = ((), (), s32[]{:S(2)}) async-start(), calls=%async_computation.1 | async-start | bytes 3538944 | tf_op jit(solution)/shard_map/all_gather | solution.py:8
  7.3 53.0 %all-gather.7.cloned.1.call-start = ((), (), s32[]{:S(2)}) async-start(), calls=%async_computation.2 | async-start | bytes 3538944 | tf_op jit(solution)/shard_map/all_gather | solution.py:18
  8.0 70.7 %all-gather.9.cloned.1.call-start = ((), (), s32[]{:S(2)}) async-start(), calls=%async_computation.3 | async-start | bytes 3538944 | tf_op jit(solution)/shard_map/all_gather | solution.py:27
  8.1 58.4 %copy-start = (bf16[1,768,768]{2,1,0:T(8,128)(2,1)S(1)}, bf16[1,768,768]{2,1,0:T(8,128)(2,1)}, u32[]{:S(2)}) copy-start(bf16[1,768,768]{2,1,0:T(8,128)(2,1)} %param.5) | copy-start | bytes 3538948
  84.9 5.9 %copy-start.2 = (s32[96,8]{0,1:T(8,128)S(1)}, s32[96,8]{0,1:T(8,128)}, u32[]{:S(2)}) copy-start(s32[96,8]{0,1:T(8,128)} %param.7) | copy-start | bytes 9220
  84.9 34.9 %all-to-all-start = ((bf16[1,8,96,768]{3,2,0,1:T(8,128)(2,1)}), bf16[1,8,96,768]{3,2,0,1:T(8,128)(2,1)S(1)}, u32[]{:S(2)}, u32[]{:S(2)}) async-start(bf16[1,8,96,768]{3,2,0,1:T(8,128)(2,1)} %bitcast.7), calls=%async_computation | async-start | bytes 2359296 | tf_op jit(solution)/shard_map/all_to_all | solution.py:33
Sparse Core Ops, SparseCore 0:
  8.9 38.7 all-gather.4
  49.2 10.9 all-gather.6
  66.6 12.1 all-gather.8
where the time goes:
time: 135 us
  waiting for transfers between devices  94 us (70%)
  between operations  13.2 us (10%)
  matrix products  12.3 us (9%)
  local copies, waits for them, and re-layouts  9.52 us (7%)
  starting transfers between devices  5.99 us (4%)
    all_gather x1, waiting for transfers between devices, on_device(): left_full = lax.all_gather(left_part, 'col', axis=2, tiled=True)  39.6 us
    all_to_all x1, waiting for transfers between devices, on_device(): lax.all_to_all(summed, 'mom', split_axis=1, concat_axis=0, tiled=True)  28.8 us
    all_gather x1, waiting for transfers between devices, on_device(): lax.all_gather(vertex, 'row', axis=1, tiled=True)  12.5 us
    all_gather x1, waiting for transfers between devices, on_device(): lax.all_gather(first_round, 'row', axis=2, tiled=True)  11.6 us
    gather x1, local copies, waits for them, and re-layouts, on_device(): return regrouped[cross_map, which]  8.68 us
    dot_general x1, matrix products, on_device(): jnp.einsum('qkb,qak->qba', lax.all_gather(vertex, 'row', axis=1, tiled=Tr...  6.21 us
    dot_general x1, matrix products, on_device(): jnp.einsum('qbk,qak->qba', lax.all_gather(first_round, 'row', axis=2, til...  6.14 us
    all_to_all x1, starting transfers between devices, on_device(): lax.all_to_all(summed, 'mom', split_axis=1, concat_axis=0, tiled=True)  5.91 us
  transfers between devices with their start and end apart: 4, of which 4 were waited for; matrix products, arithmetic and copies ran while one was open for 1% of the time, Pallas kernels for 0%

commit v1 on v0

--- a/solution.py
+++ b/solution.py
@@ -30,7 +30,10 @@
     )
     summed = (flipped + first_term + second_term).astype(jnp.bfloat16)
     summed = summed.reshape(local_q, momenta, per_device, row_count)
-    received = lax.all_to_all(summed, "mom", split_axis=1, concat_axis=0, tiled=True)
+    received = jnp.concatenate(
+        lax.all_to_all(jnp.stack(jnp.split(summed, lax.axis_size("mom"), axis=1)), "mom", 0, 0),
+        axis=0,
+    )
     regrouped = received.reshape(-1, per_device, received.shape[-1])
     which = jnp.arange(per_device, dtype=jnp.int32)[:, None]
     return regrouped[cross_map, which]

time: 135 us -> 140 us (1.037)
  local copies, waits for them, and re-layouts: 9.52 us -> 16.1 us
    unnamed x7 -> x14, local copies, waits for them, and re-layouts: 0.66 us -> 6.58 us
where the time goes in v1:
time: 140 us; the launch traced here: 139 us
  waiting for transfers between devices  92.8 us (66%)
  local copies, waits for them, and re-layouts  16.1 us (12%)
  between operations  13.2 us (9%)
  matrix products  11.3 us (8%)
  starting transfers between devices  5.99 us (4%)
    all_gather x1, waiting for transfers between devices, on_device(): left_full = lax.all_gather(left_part, 'col', axis=2, tiled=True)  39.6 us
    all_to_all x1, waiting for transfers between devices, on_device(): lax.all_to_all(jnp.stack(jnp.split(summed, lax.axis_size('mom'), axis=1))...  28.8 us
    all_gather x1, waiting for transfers between devices, on_device(): lax.all_gather(vertex, 'row', axis=1, tiled=True)  12.5 us
    all_gather x1, waiting for transfers between devices, on_device(): lax.all_gather(first_round, 'row', axis=2, tiled=True)  10.4 us
    gather x1, local copies, waits for them, and re-layouts, on_device(): return regrouped[cross_map, which]  8.68 us
    unnamed x14, local copies, waits for them, and re-layouts  6.58 us
    dot_general x1, matrix products, on_device(): jnp.einsum('qkb,qak->qba', lax.all_gather(vertex, 'row', axis=1, tiled=Tr...  6.21 us
    all_to_all x1, starting transfers between devices, on_device(): lax.all_to_all(jnp.stack(jnp.split(summed, lax.axis_size('mom'), axis=1))...  5.91 us
  transfers between devices with their start and end apart: 4, of which 4 were waited for; matrix products, arithmetic and copies ran while one was open for 1% of the time, Pallas kernels for 0%

profile of v1, /device:TPU:0, one launch (start us, length us, event | category | flops | bytes accessed | tf_op | source)
XLA Modules:
  0.0 139.4 jit_solution(2156824598119331627)
XLA Ops:
  6.5 0.0 copy-start.1
  6.5 0.0 all-gather.5.cloned.1.call-start
  6.5 0.7 all-gather.5.cloned.1.call-update
  7.3 0.0 all-gather.7.cloned.1.call-start
  7.3 0.7 all-gather.7.cloned.1.call-update
  8.0 0.0 all-gather.9.cloned.1.call-start
  8.1 0.0 copy-done.1
  8.1 39.6 %all-gather.5.cloned.1.call-done = bf16[1,768,1536]{2,1,0:T(8,128)(2,1)} async-done(((bf16[1,768,768]{2,1,0:T(8,128)(2,1)}), bf16[1,768,1536]{2,1,0:T(8,128)(2,1)}) %all-gather.5.cloned.1.call-update) | async-done | bytes 2359312 | tf_op jit(solution)/shard_map/all_gather | solution.py:8
  47.7 12.5 %all-gather.7.cloned.1.call-done = bf16[1,1536,768]{2,1,0:T(8,128)(2,1)} async-done(((bf16[1,768,768]{2,1,0:T(8,128)(2,1)}), bf16[1,1536,768]{2,1,0:T(8,128)(2,1)}) %all-gather.7.cloned.1.call-update) | async-done | bytes 2359312 | tf_op jit(solution)/shard_map/all_gather | solution.py:18
  60.2 6.2 %bitcast_convert_fusion = (bf16[768,768]{1,0:T(8,128)(2,1)}, f32[768,768]{0,1:T(8,128)}) fusion(bf16[1,1536,768]{2,1,0:T(8,128)(2,1)} %all-gather.7.cloned.1.call-done, bf16[1,768,1536]{2,1,0:T(8,128)(2,1)} %all-gather.5.cloned.1.call-done, f32[1536]{0:T(1024)S(1)} %reduce), kind=kOutput, calls=%fused_computation.6 | convolution fusion | flops 1816068096 | bytes 8263680 | tf_op jit(solution)/shard_map/qkb,qak->qba/dot_general | solution.py:16
  66.4 0.0 copy-start
  66.4 0.0 all-gather.9.cloned.1.call-update
  66.5 1.2 copy-done
  67.7 0.6 copy.22
  68.3 10.4 %all-gather.9.cloned.1.call-done = bf16[768,1536]{1,0:T(8,128)(2,1)} async-done(((bf16[768,768]{1,0:T(8,128)(2,1)}), bf16[768,1536]{1,0:T(8,128)(2,1)}) %all-gather.9.cloned.1.call-update) | async-done | bytes 2359312 | tf_op jit(solution)/shard_map/all_gather | solution.py:27
  78.7 5.1 %fusion.2 = bf16[1,768,768]{2,1,0:T(8,128)(2,1)S(1)} fusion(f32[768,768]{0,1:T(8,128)} %get-tuple-element.6, bf16[1,768,768]{1,2,0:T(8,128)(2,1)S(1)} %copy.22, bf16[768,1536]{1,0:T(8,128)(2,1)} %all-gather.9.cloned.1.call-done, bf16[1,768,1536]{2,1,0:T(8,128)(2,1)} %all-gather.5.cloned.1.call-done, f32[1536]{0:T(1024)S(1)} %reduce), kind=kOutput, calls=%fused_computation.5 | convolution fusion | flops 1817837568 | bytes 9443328 | tf_op jit(solution)/shard_map/qbk,qak->qba/dot_general | solution.py:25
  83.9 0.7 fusion.17
  84.5 0.7 fusion.16
  85.2 0.7 fusion.15
  85.9 0.7 fusion.14
  86.6 0.7 fusion.13
  87.2 0.7 fusion.12
  87.9 0.7 fusion.11
  88.6 0.7 fusion.10
  89.2 0.0 copy-start.2
  89.2 5.9 %all-to-all-start = ((bf16[8,1,1,96,768]{4,3,2,1,0:T(8,128)(2,1)}), bf16[8,1,1,96,768]{4,3,2,1,0:T(8,128)(2,1)S(1)}, u32[]{:S(2)}, u32[]{:S(2)}) async-start(bf16[8,1,1,96,768]{4,3,2,1,0:T(8,128)(2,1)} %fusion.10), calls=%async_computation | async-start | bytes 2359296 | tf_op jit(solution)/shard_map/all_to_all | solution.py:34
  95.2 0.0 copy-done.2
  95.2 0.1 copy.23
  95.3 0.1 reshape.25
  95.4 28.8 %all-to-all-done = bf16[8,1,1,96,768]{4,3,2,1,0:T(8,128)(2,1)S(1)} async-done(((bf16[8,1,1,96,768]{4,3,2,1,0:T(8,128)(2,1)}), bf16[8,1,1,96,768]{4,3,2,1,0:T(8,128)(2,1)S(1)}, u32[]{:S(2)}, u32[]{:S(2)}) %all-to-all-start) | async-done | bytes 1179680 | tf_op jit(solution)/shard_map/all_to_all | solution.py:34
  124.2 8.7 %gather_fusion = bf16[768,768]{1,0:T(8,128)(2,1)} fusion(bf16[8,96,768]{2,1,0:T(8,128)(2,1)S(1)} %bitcast.68, s32[768]{0:T(1024)S(1)} %reshape.25), kind=kCustom, calls=%fused_computation | custom fusion | bytes 2365440 | tf_op jit(solution)/shard_map/gather | solution.py:39
  (2 shorter events, 0.0 us)
Async XLA Ops:
  6.5 1.5 %copy-start.1 = (f32[1,1536]{1,0:T(1,128)S(1)}, f32[1,1536]{1,0:T(1,128)}, u32[]{:S(2)}) copy-start(f32[1,1536]{1,0:T(1,128)} %param.6) | copy-start | bytes 18436
  6.5 41.1 %all-gather.5.cloned.1.call-start = ((), (), s32[]{:S(2)}) async-start(), calls=%async_computation.1 | async-start | bytes 3538944 | tf_op jit(solution)/shard_map/all_gather | solution.py:8
  7.3 53.0 %all-gather.7.cloned.1.call-start = ((), (), s32[]{:S(2)}) async-start(), calls=%async_computation.2 | async-start | bytes 3538944 | tf_op jit(solution)/shard_map/all_gather | solution.py:18
  8.0 70.7 %all-gather.9.cloned.1.call-start = ((), (), s32[]{:S(2)}) async-start(), calls=%async_computation.3 | async-start | bytes 3538944 | tf_op jit(solution)/shard_map/all_gather | solution.py:27
  66.4 1.3 copy-start
  89.2 5.9 %copy-start.2 = (s32[96,8]{0,1:T(8,128)S(1)}, s32[96,8]{0,1:T(8,128)}, u32[]{:S(2)}) copy-start(s32[96,8]{0,1:T(8,128)} %param.7) | copy-start | bytes 9220
  89.2 34.9 %all-to-all-start = ((bf16[8,1,1,96,768]{4,3,2,1,0:T(8,128)(2,1)}), bf16[8,1,1,96,768]{4,3,2,1,0:T(8,128)(2,1)S(1)}, u32[]{:S(2)}, u32[]{:S(2)}) async-start(bf16[8,1,1,96,768]{4,3,2,1,0:T(8,128)(2,1)} %fusion.10), calls=%async_computation | async-start | bytes 2359296 | tf_op jit(solution)/shard_map/all_to_all | solution.py:34
Sparse Core Ops, SparseCore 0:
  8.9 38.7 all-gather.4
  49.2 10.9 all-gather.6
  66.6 12.1 all-gather.8
